TPU v7x, 32 devices: a whole 2x2x4 slice. The times are simulated.
32 devices in a mesh: tissue: 2 (over x), sample: 4 (over y, core), variant: 4 (over z).
Axes of the slice: x: 2, y: 2, z: 4, core: 2. Of those that a mesh axis runs over, the one named last changes fastest.
Arguments:
- dosage: bfloat16 [52, 512, 512], P('tissue', 'sample', 'variant'), may hold values from 0 to 2
- express: bfloat16 [52, 512, 2048], P('tissue', 'sample', 'variant'), may hold values from -6 to 6
- covar: float32 [52, 32, 512], P('tissue', None, 'sample'), may hold values from -6 to 6
- member: int32 [52, 512], P('tissue', 'sample'), may hold values 0 or 1
- live: int32 [52], replicated, may hold values 0 or 1
- mixing: float32 [52, 52], replicated, may hold values from -1 to 2, as said below
Outputs:
- chi_stat: float32 [512, 2048], P('variant', 'sample')
- meta_stat: float32 [512, 2048], P('variant', 'sample')
Inputs may be any that keep to these rules, and one draw needn't show every extreme that they name: mixing is the identity plus a dense spread of off-diagonal and diagonal terms.
All inputs are finite; a program needn't handle non-finite values. No bound on the sum of `member` on one device may be relied on, other than what follows from the above.
Results may differ from a plain program's by a relative error of at most 0.019.
Values may be sent and summed in bfloat16 or wider, within the bound.
A program may use at most 128 MiB of HBM per device.

v0:
```python
import jax
import jax.numpy as jnp
from jax import lax
from jax.sharding import PartitionSpec as P


def solve_small(factor_low, rhs_matrix):
    forward = lax.linalg.triangular_solve(factor_low, rhs_matrix, left_side=True, lower=True)
    return lax.linalg.triangular_solve(
        factor_low, forward, left_side=True, lower=True, transpose_a=True
    )


def body(dosage, express, covar, member, live, mixing):
    highest = lax.Precision.HIGHEST
    tis_dev = dosage.shape[0]
    n_cov = covar.shape[1]
    weights = member.astype(jnp.float32)
    dos_masked = dosage.astype(jnp.float32) * weights[:, :, None]
    cov_masked = covar * weights[:, None, :]
    gram_part = jnp.einsum("tks,tjs->tkj", cov_masked, cov_masked, precision=highest)
    amat_part = jnp.einsum("tks,tsv->tkv", cov_masked, dos_masked, precision=highest)
    count_part = jnp.sum(weights, axis=1)
    gsq_part = jnp.sum(dos_masked * dos_masked, axis=1)
    identity = jnp.eye(n_cov, dtype=jnp.float32)
    gathered = lax.all_gather(express, "variant", axis=2, tiled=True)
    exp_masked = gathered.astype(jnp.float32) * weights[:, :, None]
    bmat_part = jnp.einsum("tks,tsg->tkg", cov_masked, exp_masked, precision=highest)
    esq_part = jnp.sum(exp_masked * exp_masked, axis=1)
    gram_sum, amat_sum, counts, gsq_sum, bmat_sum, esq_sum = (
        lax.psum(gram_part.astype(jnp.bfloat16), "sample").astype(jnp.float32),
        lax.psum(amat_part.astype(jnp.bfloat16), "sample").astype(jnp.float32),
        lax.psum(count_part.astype(jnp.bfloat16), "sample").astype(jnp.float32),
        lax.psum(gsq_part.astype(jnp.bfloat16), "sample").astype(jnp.float32),
        lax.psum(bmat_part.astype(jnp.bfloat16), "sample").astype(jnp.float32),
        lax.psum(esq_part.astype(jnp.bfloat16), "sample").astype(jnp.float32),
    )
    factor_low = jnp.linalg.cholesky(gram_sum + identity)
    proj_exp = solve_small(factor_low, bmat_sum)
    eres = (
        exp_masked - jnp.einsum("tks,tkg->tsg", cov_masked, proj_exp, precision=highest)
    ).astype(jnp.bfloat16)
    enorm = esq_sum - jnp.sum(bmat_sum * proj_exp, axis=1)
    proj_dos = solve_small(factor_low, amat_sum)
    gres = (
        dos_masked - jnp.einsum("tks,tkv->tsv", cov_masked, proj_dos, precision=highest)
    ).astype(jnp.bfloat16)
    gnorm = gsq_sum - jnp.sum(amat_sum * proj_dos, axis=1)
    n_genes = eres.shape[2]
    gene_share = n_genes // lax.axis_size("sample")
    cross = lax.psum_scatter(
        jnp.einsum("tse,tsv->etv", eres, gres, preferred_element_type=jnp.float32).astype(
            jnp.bfloat16
        ),
        "sample",
        scatter_dimension=0,
        tiled=True,
    ).astype(jnp.float32)
    gene_start = lax.axis_index("sample") * gene_share
    enorm_slice = lax.dynamic_slice_in_dim(enorm, gene_start, gene_share, 1)
    tissue_start = lax.axis_index("tissue") * tis_dev
    live_f = live.astype(jnp.float32)
    live_own = lax.dynamic_slice_in_dim(live_f, tissue_start, tis_dev, 0)
    scales = live_own * jnp.sqrt(jnp.maximum(counts - n_cov, 1.0))
    inv_var = 1.0 / jnp.sqrt(gnorm + 1e-05)
    inv_gene = 1.0 / jnp.sqrt(enorm_slice + 1e-05)
    zvals = (
        cross * scales[None, :, None] * inv_var[None, :, :] * jnp.transpose(inv_gene)[:, :, None]
    )
    own_rows = lax.dynamic_slice_in_dim(mixing, tissue_start, tis_dev, 0)
    mixed = jnp.zeros_like(zvals) + jnp.einsum(
        "ut,gtv->guv",
        own_rows,
        lax.all_gather(zvals.astype(jnp.bfloat16), "tissue", axis=1, tiled=True).astype(
            jnp.float32
        ),
        precision=highest,
    )
    mixed = mixed * live_own[None, :, None]
    nlive = jnp.maximum(jnp.sum(live_f), 1.0)
    chi_part = jnp.sum(mixed * mixed, axis=1) / nlive
    meta_part = jnp.sum(mixed, axis=1) / jnp.sqrt(nlive)
    chi_stat, meta_stat = (
        lax.psum(chi_part.astype(jnp.bfloat16), "tissue").astype(jnp.float32),
        lax.psum(meta_part.astype(jnp.bfloat16), "tissue").astype(jnp.float32),
    )
    return (jnp.transpose(chi_stat), jnp.transpose(meta_stat))


def solution(mesh):
    return jax.shard_map(
        body,
        mesh=mesh,
        in_specs=(
            P("tissue", "sample", "variant"),
            P("tissue", "sample", "variant"),
            P("tissue", None, "sample"),
            P("tissue", "sample"),
            P(),
            P(),
        ),
        out_specs=(P("variant", "sample"), P("variant", "sample")),
        check_vma=False,
    )
```

profile of v0, /device:TPU:0, one launch (start us, length us, event | category | flops | bytes accessed | tf_op | source)
XLA Modules:
  0.0 741.3 jit_solution(18436027038904383437)
XLA Ops:
  7.2 0.7 all-gather.3.cloned.1.call-update
  8.0 0.7 convert_element_type.83
  8.7 3.7 fusion.8
  12.4 235.3 %all-gather.3.cloned.1.call-done = bf16[26,128,2048]{2,1,0:T(8,128)(2,1)} async-done(((bf16[26,128,512]{2,1,0:T(8,128)(2,1)}), bf16[26,128,2048]{2,1,0:T(8,128)(2,1)}) %all-gather.3.cloned.1.call-update) | async-done | bytes 13631504 | tf_op jit(solution)/shard_map/all_gather | solution.py:26
  247.6 19.7 %fusion.6 = bf16[26,32,2048]{2,1,0:T(8,128)(2,1)} fusion(bf16[26,128,2048]{2,1,0:T(8,128)(2,1)} %all-gather.3.cloned.1.call-done, f32[26,128]{1,0:T(8,128)S(1)} %convert_element_type.83, f32[26,32,128]{2,1,0:T(8,128)} %param.8), kind=kOutput, calls=%fused_computation.14 | convolution fusion | flops 2632687616 | bytes 17478656 | tf_op jit(solution)/shard_map/tks,tsg->tkg/dot_general | solution.py:28
  267.4 10.8 %multiply_reduce_fusion = bf16[26,2048]{1,0:T(8,128)(2,1)} fusion(bf16[26,128,2048]{2,1,0:T(8,128)(2,1)} %all-gather.3.cloned.1.call-done, f32[26,128]{1,0:T(8,128)S(1)} %convert_element_type.83), kind=kLoop, calls=%fused_computation | loop fusion | flops 27209728 | bytes 13751296 | tf_op jit(solution)/shard_map/reduce_sum | solution.py:29
  278.2 0.3 reduce-scatter.2.cloned.1.call-start
  278.7 0.5 multiply_reduce_fusion.2
  279.2 0.8 convolution_convert_fusion.1
  280.0 19.6 %all-reduce = (bf16[26,32,32]{1,2,0:T(8,128)(2,1)S(1)}, bf16[26,128]{1,0:T(8,128)(2,1)S(1)}, bf16[26]{0:T(256)(128)(2,1)S(1)}) all-reduce(bf16[26,32,32]{1,2,0:T(8,128)(2,1)S(1)} %convolution_convert_fusion.1, bf16[26,128]{1,0:T(8,128)(2,1)S(1)} %multiply_reduce_fusion.2, ...), channel_id=1, replica_groups=mesh['tissue'=2,'sample'=4,'variant'=4] {'sample'}, use_global_device_ids=true, to_apply=%region_0.0 | all-reduce | flops 29978 | bytes 119912 | tf_op jit(solution)/shard_map/psum | solution.py:31
  299.6 0.2 copy.19
  299.9 76.2 %custom-call.13 = f32[26,32,32]{2,1,0:T(8,128)S(1)} custom-call(f32[26,32,32]{2,1,0:T(8,128)S(1)} %fusion.18), custom_call_target="Cholesky" | custom-call | tf_op jit(solution)/shard_map/jit(cholesky)/cholesky | solution.py:38
  376.4 64.7 %custom-call.14 = f32[26,1,32,32]{2,3,1,0:T(8,128)} custom-call(f32[26,1,32,32]{3,2,1,0:T(8,128)S(1)} %select_bitcast_fusion), custom_call_target="InvertDiagBlocksLowerTriangular" | custom-call | tf_op jit(solution)/shard_map/triangular_solve | solution.py:9
  441.2 5.2 fusion.12
  446.5 8.4 %multiply_reduce_fusion.1 = (f32[26,2048]{1,0:T(8,128)}, f32[26,32,2048]{2,1,0:T(8,128)S(1)}) fusion(bf16[26,32,2048]{2,1,0:T(8,128)(2,1)S(1)} %copy-done.3, f32[26,32,2048]{2,1,0:T(8,128)S(1)} %fusion.12, f32[26,1,32,32]{2,3,1,0:T(8,128)S(1)} %copy-done.6), kind=kOutput, calls=%fused_computation.13 | convolution fusion | flops 659369984 | bytes 17358848 | tf_op jit(solution)/shard_map/triangular_solve | solution.py:9
  454.8 0.5 fusion.16
  455.3 0.6 multiply_reduce_fusion.3
  456.0 3.6 subtract_convert_fusion.1
  459.6 27.0 %subtract_convert_fusion = bf16[26,128,2048]{2,1,0:T(8,128)(2,1)} fusion(bf16[26,128,2048]{2,1,0:T(8,128)(2,1)S(1)} %bitcast.46, f32[26,32,2048]{2,1,0:T(8,128)S(1)} %get-tuple-element.19, f32[26,128]{1,0:T(8,128)S(1)} %convert_element_type.83, f32[26,32,128]{2,1,0:T(8,128)} %param.8), kind=kOutput, calls=%fused_computation.1 | convolution fusion | flops 2644615168 | bytes 34518016 | tf_op jit(solution)/shard_map/tks,tkg->tsg/dot_general | solution.py:41
  486.6 13.5 %fusion.2 = bf16[2048,26,128]{0,2,1:T(8,128)(2,1)} fusion(bf16[26,128,128]{2,1,0:T(8,128)(2,1)S(1)} %subtract_convert_fusion.1, bf16[26,128,2048]{2,1,0:T(8,128)(2,1)} %subtract_convert_fusion), kind=kOutput, calls=%fused_computation.6 | convolution fusion | flops 1751646208 | bytes 28114944 | tf_op jit(solution)/shard_map/tse,tsv->etv/dot_general | solution.py:52
  500.2 0.6 copy-done.9
  500.9 0.9 fusion.33
  501.7 99.4 %reduce-scatter.2.cloned.1.call-done = bf16[512,26,128]{0,2,1:T(8,128)(2,1)} async-done(((bf16[2048,26,128]{0,2,1:T(8,128)(2,1)}), bf16[512,26,128]{0,2,1:T(8,128)(2,1)}) %reduce-scatter.2.cloned.1.call-update) | async-done | bytes 3407888 | tf_op jit(solution)/shard_map/reduce_scatter | solution.py:51
  601.1 2.8 multiply_convert_fusion
  604.0 3.6 copy.23
  607.6 0.6 convert_reduce_fusion
  608.9 85.1 %all-gather.5.cloned.1.call-done = bf16[512,52,128]{2,0,1:T(8,128)(2,1)} async-done(((bf16[512,26,128]{2,0,1:T(8,128)(2,1)}), bf16[512,52,128]{2,0,1:T(8,128)(2,1)}) %all-gather.5.cloned.1.call-update) | async-done | bytes 6815760 | tf_op jit(solution)/shard_map/all_gather | solution.py:74
  694.0 12.9 %bitcast_reduce_fusion = (f32[512,128]{1,0:T(8,128)S(1)}, f32[512,128]{1,0:T(8,128)S(1)}) fusion(f32[26]{0:T(128)S(1)} %get-tuple-element.17, f32[52,52]{1,0:T(8,128)S(1)} %copy-done, s32[]{:T(128)S(6)} %select_n.12, bf16[512,52,128]{2,0,1:T(8,128)(2,1)} %all-gather.5.cloned.1.call-done), kind=kOutput, calls=%fused_computation.7 | convolution fusion | flops 1069940736 | bytes 7356932 | tf_op jit(solution)/shard_map/ut,gtv->guv/dot_general | solution.py:71
  706.9 0.8 fusion.29
  707.7 23.5 %all-reduce.8.cloned.1.call-done = (bf16[128,512]{0,1:T(8,128)(2,1)}, bf16[128,512]{0,1:T(8,128)(2,1)}) async-done(((bf16[128,512]{0,1:T(8,128)(2,1)}, bf16[128,512]{0,1:T(8,128)(2,1)}), (bf16[128,512]{0,1:T(8,128)(2,1)}, bf16[128,512]{0,1:T(8,128)(2,1)})) %all-reduce.8.cloned.1.call-update) | async-done | bytes 262160 | tf_op jit(solution)/shard_map/psum | solution.py:84
  731.2 1.7 copy.25
  732.9 1.7 copy.26
  (50 shorter events, 1.0 us)
Async XLA Ops:
  7.2 686.8 %copy-start = (f32[52,52]{1,0:T(8,128)S(1)}, f32[52,52]{1,0:T(8,128)}, u32[]{:S(2)}) copy-start(f32[52,52]{1,0:T(8,128)} %param.11) | copy-start | bytes 32452
  7.2 240.5 %all-gather.3.cloned.1.call-start = ((), (), s32[]{:S(2)}) async-start(), calls=%async_computation.1 | async-start | bytes 17039360 | tf_op jit(solution)/shard_map/all_gather | solution.py:26
  7.9 433.2 %all-reduce.6.cloned.1.call-start = ((), (), s32[]{:S(2)}) async-start(), calls=%async_computation.4 | async-start | bytes 7503872 | tf_op jit(solution)/shard_map/psum | solution.py:32
  267.4 11.2 %copy-start.8 = (s32[26,128]{1,0:T(8,128)S(1)}, s32[26,128]{1,0:T(8,128)}, u32[]{:S(2)}) copy-start(s32[26,128]{1,0:T(8,128)} %param.9) | copy-start | bytes 39940
  267.4 11.3 %copy-start.4 = (bf16[26,128,128]{2,1,0:T(8,128)(2,1)S(1)}, bf16[26,128,128]{2,1,0:T(8,128)(2,1)}, u32[]{:S(2)}) copy-start(bf16[26,128,128]{2,1,0:T(8,128)(2,1)} %param.6) | copy-start | bytes 2555908
  267.4 11.8 %copy-start.1 = (f32[26,32,128]{2,1,0:T(8,128)S(1)}, f32[26,32,128]{2,1,0:T(8,128)}, u32[]{:S(2)}) copy-start(f32[26,32,128]{2,1,0:T(8,128)} %param.8) | copy-start | bytes 1277956
  278.2 323.0 %reduce-scatter.2.cloned.1.call-start = ((), (), s32[]{:S(2)}) async-start(), calls=%async_computation.2 | async-start | bytes 17039360 | tf_op jit(solution)/shard_map/reduce_scatter | solution.py:51
  441.1 5.2 copy-start.3
  441.1 5.3 copy-start.6
  441.1 18.4 %slice-start = ((s8[13631488]{0:T(1024)(128)(4,1)}), s8[4194304]{0:T(1024)(128)(4,1)S(1)}, s32[]{:S(2)}) async-start(s8[13631488]{0:T(1024)(128)(4,1)} %bitcast.45), calls=%async_computation.6 | async-start | bytes 8388608
  441.2 18.4 %slice-start.1 = ((s8[13631488]{0:T(1024)(128)(4,1)}), s8[4194304]{0:T(1024)(128)(4,1)S(1)}, s32[]{:S(2)}) async-start(s8[13631488]{0:T(1024)(128)(4,1)} %bitcast.45), calls=%async_computation.7 | async-start | bytes 8388608
  446.4 8.4 %copy-start.7 = (bf16[26,32,128]{2,1,0:T(8,128)(2,1)S(1)}, bf16[26,32,128]{2,1,0:T(8,128)(2,1)}, u32[]{:S(2)}) copy-start(bf16[26,32,128]{2,1,0:T(8,128)(2,1)} %get-tuple-element.11) | copy-start | bytes 638980
  446.4 9.5 %copy-start.2 = (f32[26,32,128]{2,1,0:T(8,128)S(1)}, f32[26,32,128]{2,1,0:T(8,128)}, u32[]{:S(2)}) copy-start(f32[26,32,128]{2,1,0:T(8,128)} %param.8) | copy-start | bytes 1277956
  446.4 9.5 %copy-start.5 = (bf16[26,128,128]{2,1,0:T(8,128)(2,1)S(1)}, bf16[26,128,128]{2,1,0:T(8,128)(2,1)}, u32[]{:S(2)}) copy-start(bf16[26,128,128]{2,1,0:T(8,128)(2,1)} %param.6) | copy-start | bytes 2555908
  446.4 13.1 %slice-start.2 = ((s8[13631488]{0:T(1024)(128)(4,1)}), s8[4194304]{0:T(1024)(128)(4,1)S(1)}, s32[]{:S(2)}) async-start(s8[13631488]{0:T(1024)(128)(4,1)} %bitcast.45), calls=%async_computation.8 | async-start | bytes 8388608
  446.5 13.1 %slice-start.3 = ((s8[13631488]{0:T(1024)(128)(4,1)}), s8[1048576]{0:T(1024)(128)(4,1)S(1)}, s32[]{:S(2)}) async-start(s8[13631488]{0:T(1024)(128)(4,1)} %bitcast.45), calls=%async_computation.9 | async-start | bytes 2097152
  500.1 0.7 copy-start.9
  500.2 193.8 %all-gather.5.cloned.1.call-start = ((), (), s32[]{:S(2)}) async-start(), calls=%async_computation.3 | async-start | bytes 10223616 | tf_op jit(solution)/shard_map/all_gather | solution.py:74
  607.6 123.6 %all-reduce.8.cloned.1.call-start = ((), (), s32[]{:S(2)}) async-start(), calls=%async_computation.5 | async-start | bytes 524288 | tf_op jit(solution)/shard_map/psum | solution.py:84
Sparse Core Ops, SparseCore 0:
  9.6 238.0 all-gather.2
  278.3 79.3 all-reduce.5
  500.3 100.8 reduce-scatter.1
  607.7 86.2 all-gather.4
  707.8 23.3 all-reduce.7
where the time goes:
time: 755 us; the launch traced here: 741 us
  waiting for transfers between devices  444 us (59%)
  other arithmetic  159 us (21%)
  matrix products  95.9 us (13%)
  blocking collectives  19.6 us (3%)
  between operations  15 us (2%)
  local copies, waits for them, and re-layouts  7.88 us (1%)
    all_gather x1, waiting for transfers between devices, body(): gathered = lax.all_gather(express, 'variant', axis=2, tiled=True)  235 us
    reduce_scatter x1, waiting for transfers between devices, body(): lax.psum_scatter(jnp.einsum('tse,tsv->etv', eres, gres, preferred_element...  99.4 us
    all_gather x1, waiting for transfers between devices, body(): lax.all_gather(zvals.astype(jnp.bfloat16), 'tissue', axis=1, tiled=True)  85.1 us
    another operation x4, other arithmetic, body(): factor_low = jnp.linalg.cholesky(gram_sum + identity)  76.4 us
    another operation x3, other arithmetic, solve_small(): lax.linalg.triangular_solve(factor_low, forward, left_side=True, lower=Tr...  64.9 us
    dot_general x1, matrix products, body(): jnp.einsum('tks,tkg->tsg', cov_masked, proj_exp, precision=highest)  27 us
    psum x1, waiting for transfers between devices, body(): lax.psum(chi_part.astype(jnp.bfloat16), 'tissue').astype(jnp.float32)  23.5 us
    dot_general x1, matrix products, body(): jnp.einsum('tks,tsg->tkg', cov_masked, exp_masked, precision=highest)  19.7 us
  transfers between devices with their start and end apart: 5, of which 4 were waited for; matrix products, arithmetic and copies ran while one was open for 20% of the time, Pallas kernels for 0%

commit v1 on v0

v1 whole, which is shorter than its diff:
```python
import jax
import jax.numpy as jnp
from jax import lax
from jax.experimental import pallas as pl
from jax.experimental.pallas import tpu as pltpu
from jax.sharding import PartitionSpec as P

HIGHEST = lax.Precision.HIGHEST


def invert_kernel(gram_ref, out_ref):
    n = gram_ref.shape[0]
    lanes = gram_ref.shape[2]
    eye = (
        lax.broadcasted_iota(jnp.int32, (n, n, lanes), 0)
        == lax.broadcasted_iota(jnp.int32, (n, n, lanes), 1)
    ).astype(jnp.float32)
    out_ref[...] = gram_ref[...] + eye
    row_ids = lax.broadcasted_iota(jnp.int32, (n, lanes), 0)

    def step(k, carry):
        pivot = 1.0 / out_ref[k, pl.ds(k, 1), :]
        here = row_ids == k
        row = jnp.where(here, pivot, out_ref[k] * pivot)
        col = out_ref[:, pl.ds(k, 1), :]
        out_ref[...] = jnp.where(here[None], 0.0, out_ref[...]) - col * row[None]
        out_ref[k] = row
        return carry

    lax.fori_loop(0, n, step, 0)


def invert(gram):
    tis, n, _ = gram.shape
    lanes = -(-tis // 128) * 128
    packed = jnp.pad(jnp.transpose(gram, (1, 2, 0)), ((0, 0), (0, 0), (0, lanes - tis)))
    out = pl.pallas_call(
        invert_kernel,
        out_shape=jax.ShapeDtypeStruct((n, n, lanes), jnp.float32),
        name="invert_gram",
    )(packed)
    return jnp.transpose(out[:, :, :tis], (2, 0, 1))


def body(dosage, express, covar, member, live, mixing):
    tis_dev = dosage.shape[0]
    n_cov = covar.shape[1]
    n_x = lax.axis_size("tissue")
    n_s = lax.axis_size("sample")
    n_v = lax.axis_size("variant")
    ix = lax.axis_index("tissue")
    i_s = lax.axis_index("sample")
    i_v = lax.axis_index("variant")
    weights = member.astype(jnp.float32)
    dos_m = dosage.astype(jnp.float32) * weights[:, :, None]
    cov_m = covar * weights[:, None, :]
    exp_m = express.astype(jnp.float32) * weights[:, :, None]
    parts = (
        jnp.einsum("tks,tjs->tkj", cov_m, cov_m, precision=HIGHEST),
        jnp.einsum("tks,tsv->tkv", cov_m, dos_m, precision=HIGHEST),
        jnp.einsum("tks,tsg->tkg", cov_m, exp_m, precision=HIGHEST),
        jnp.sum(dos_m * dos_m, axis=1),
        jnp.sum(exp_m * exp_m, axis=1),
        jnp.sum(weights, axis=1),
    )
    gram, amat, bmat, gsq, esq, counts = (
        part.astype(jnp.float32)
        for part in lax.psum(tuple(part.astype(jnp.bfloat16) for part in parts), "sample")
    )
    inverse = invert(gram)
    pa = jnp.einsum("tkj,tjv->tkv", inverse, amat, precision=HIGHEST)
    pb = jnp.einsum("tkj,tjg->tkg", inverse, bmat, precision=HIGHEST)
    gnorm = gsq - jnp.sum(amat * pa, axis=1)
    enorm = esq - jnp.sum(bmat * pb, axis=1)
    live_f = live.astype(jnp.float32)
    live_own = lax.dynamic_slice_in_dim(live_f, ix * tis_dev, tis_dev, 0)
    scales = live_own * jnp.sqrt(jnp.maximum(counts - n_cov, 1.0))
    inv_var = 1.0 / jnp.sqrt(gnorm + 1e-05)
    inv_gene = scales[:, None] / jnp.sqrt(enorm + 1e-05)
    gres = dos_m - jnp.einsum("tks,tkv->tsv", cov_m, pa, precision=HIGHEST)
    gres = (gres * inv_var[:, None, :]).astype(jnp.bfloat16)
    eres = exp_m - jnp.einsum("tks,tkg->tsg", cov_m, pb, precision=HIGHEST)
    eres = (eres * inv_gene[:, None, :]).astype(jnp.bfloat16)
    gathered = lax.all_gather(gres, "variant", axis=0)
    part = jnp.einsum(
        "ntsv,tsg->ntvg", gathered, eres, preferred_element_type=jnp.float32
    ).astype(jnp.bfloat16)
    part = part.reshape((n_v * tis_dev,) + part.shape[2:])
    zvals = lax.psum_scatter(part, "sample", scatter_dimension=0, tiled=True)
    zvals = zvals.reshape((n_v // n_s, tis_dev) + zvals.shape[1:])
    rows = zvals.shape[2]
    half = rows // n_x
    kept = lax.dynamic_slice_in_dim(zvals, ix * half, half, 2)
    sent = lax.dynamic_slice_in_dim(zvals, (n_x - 1 - ix) * half, half, 2)
    got = lax.ppermute(sent, "tissue", [(0, 1), (1, 0)])
    mix_own = lax.dynamic_slice_in_dim(mixing, ix * tis_dev, tis_dev, 1)
    mix_far = lax.dynamic_slice_in_dim(mixing, (n_x - 1 - ix) * tis_dev, tis_dev, 1)
    yvals = jnp.einsum(
        "ut,mtvg->umvg",
        jnp.concatenate([mix_own, mix_far], axis=1) * live_f[:, None],
        jnp.concatenate([kept, got], axis=1).astype(jnp.float32),
        precision=HIGHEST,
    )
    nlive = jnp.maximum(jnp.sum(live_f), 1.0)
    stats = jnp.stack(
        [jnp.sum(yvals * yvals, axis=0) / nlive, jnp.sum(yvals, axis=0) / jnp.sqrt(nlive)]
    ).astype(jnp.bfloat16)
    if n_s == n_v:
        near, far = [], []
        for x in range(n_x):
            for i in range(n_s):
                for j in range(n_v):
                    source = (x * n_s + i) * n_v + j
                    near.append((source, (x * n_s + j) * n_v + i))
                    far.append((source, ((n_x - 1 - x) * n_s + j) * n_v + i))
        axes = ("tissue", "sample", "variant")
        one = lax.ppermute(stats[:, 0], axes, near)
        two = lax.ppermute(stats[:, 0], axes, far)
        full = jnp.concatenate(
            [jnp.where(ix == 0, one, two), jnp.where(ix == 0, two, one)], axis=1
        )
    else:
        blocks = lax.all_gather(stats, ("tissue", "sample", "variant"), axis=0)
        blocks = blocks.reshape((n_x, n_s, n_v) + stats.shape)
        blocks = jnp.transpose(blocks, (3, 1, 4, 0, 5, 2, 6))
        whole = blocks.reshape(2, n_v * rows, n_v * stats.shape[3])
        genes = whole.shape[2] // n_s
        full = lax.dynamic_slice(whole, (0, i_v * rows, i_s * genes), (2, rows, genes))
    full = full.astype(jnp.float32)
    return (full[0], full[1])


def solution(mesh):
    return jax.shard_map(
        body,
        mesh=mesh,
        in_specs=(
            P("tissue", "sample", "variant"),
            P("tissue", "sample", "variant"),
            P("tissue", None, "sample"),
            P("tissue", "sample"),
            P(),
            P(),
        ),
        out_specs=(P("variant", "sample"), P("variant", "sample")),
        check_vma=False,
    )
```

time: 755 us -> 375 us (0.50)
  the two profiles are of different devices: /device:TPU:0 before, /device:TPU:4 now
where the time goes in v1:
time: 375 us; the launch traced here: 374 us
  waiting for transfers between devices  264 us (70%)
  matrix products  43 us (11%)
  local copies, waits for them, and re-layouts  30.2 us (8%)
  between operations  14.7 us (4%)
  other arithmetic  9.59 us (3%)
  starting transfers between devices  8.81 us (2%)
  Pallas kernels  4.27 us (1%)
    reduce_scatter x1, waiting for transfers between devices, body(): zvals = lax.psum_scatter(part, 'sample', scatter_dimension=0, tiled=True)  104 us
    all_gather x1, waiting for transfers between devices, body(): gathered = lax.all_gather(gres, 'variant', axis=0)  58.5 us
    psum x2, waiting for transfers between devices, body(): lax.psum(tuple((part.astype(jnp.bfloat16) for part in parts)), 'sample')  54.1 us
    ppermute x1, waiting for transfers between devices, body(): got = lax.ppermute(sent, 'tissue', [(0, 1), (1, 0)])  35 us
    convert_element_type x1, local copies, waits for them, and re-layouts, body(): part = jnp.einsum('ntsv,tsg->ntvg', gathered, eres, preferred_element_typ...  17.5 us
    dot_general x1, matrix products, body(): jnp.einsum('ntsv,tsg->ntvg', gathered, eres, preferred_element_type=jnp.f...  10.3 us
  transfers between devices with their start and end apart: 7, of which 7 were waited for; matrix products, arithmetic and copies ran while one was open for 7% of the time, Pallas kernels for 1%

profile of v1, /device:TPU:4, one launch (start us, length us, event | category | flops | bytes accessed | tf_op | source)
XLA Modules:
  0.0 374.2 jit_solution(18154690580498929959)
XLA Ops:
  7.2 0.9 convert_element_type.70
  8.1 1.5 convert_reduce_fusion
  9.6 2.7 convolution_convert_fusion
  12.3 1.9 copy.36
  14.2 3.4 multiply_reduce_fusion.1
  17.6 1.1 multiply_reduce_fusion.2
  18.9 6.1 %fusion.11 = bf16[26,32,512]{2,1,0:T(8,128)(2,1)} fusion(bf16[26,128,512]{2,1,0:T(8,128)(2,1)S(1)} %copy-done, f32[26,128]{1,0:T(8,128)S(1)} %convert_element_type.70, f32[26,32,128]{2,1,0:T(8,128)} %param.8), kind=kOutput, calls=%fused_computation.22 | convolution fusion | flops 658251776 | bytes 4699136 | tf_op jit(solution)/shard_map/tks,tsg->tkg/dot_general | solution.py:61
  25.0 2.4 fusion.12
  27.7 23.7 %all-reduce.6.cloned.1.call-done = (bf16[32,32,26]{2,1,0:T(8,128)(2,1)}, bf16[26,128]{1,0:T(8,128)(2,1)}, bf16[26,512]{1,0:T(8,128)(2,1)}, bf16[26]{0:T(256)(128)(2,1)}) async-done(((bf16[32,32,26]{2,1,0:T(8,128)(2,1)}, bf16[26,128]{1,0:T(8,128)(2,1)}, bf16[26,512]{1,0:T(8,128)(2,1)}, bf16[26]{0:T(256)(128)(2,1)}), (bf16[32,32,26]{2,1,0:T(8,128)(2,1)}, bf16[26,128]{1,0:T(8,128)(2,1)}, ...) | async-done | bytes 86596 | tf_op jit(solution)/shard_map/psum | solution.py:68
  51.4 1.8 pad_convert_fusion.gram_ref
  53.2 4.3 %invert_gram.1 = f32[32,32,128]{2,1,0:T(8,128)} custom-call(f32[32,32,128]{2,1,0:T(8,128)} %pad_convert_fusion.gram_ref), custom_call_target="tpu_custom_call" | custom-call | tf_op jit(solution)/shard_map/invert_gram/pallas_call | solution.py:37
  57.5 1.9 slice_bitcast_fusion
  59.4 2.2 copy.37
  61.6 30.4 %all-reduce.8.cloned.1.call-done = (bf16[26,32,512]{2,1,0:T(8,128)(2,1)}, bf16[26,32,128]{2,1,0:T(8,128)(2,1)}) async-done(((bf16[26,32,512]{2,1,0:T(8,128)(2,1)}, bf16[26,32,128]{2,1,0:T(8,128)(2,1)}), (bf16[26,32,512]{2,1,0:T(8,128)(2,1)}, bf16[26,32,128]{2,1,0:T(8,128)(2,1)})) %all-reduce.8.cloned.1.call-update) | async-done | bytes 1064976 | tf_op jit(solution)/shard_map/psum | solution.py:68
  92.0 1.5 multiply_reduce_fusion.4
  93.6 5.4 %multiply_convert_fusion.1 = bf16[26,128,128]{2,1,0:T(8,128)(2,1)} fusion(bf16[26,128,128]{2,1,0:T(8,128)(2,1)} %param.6, f32[26,32,128]{2,1,0:T(8,128)S(1)} %get-tuple-element.19, f32[26,128]{1,0:T(8,128)S(1)} %add_rsqrt_fusion, f32[26,128]{1,0:T(8,128)S(1)} %convert_element_type.70, f32[26,32,128]{2,1,0:T(8,128)} %param.8), kind=kOutput, calls=%fused_computation.17 | convolution fusion | flops 165814272 | bytes 2582528 | tf_op jit(solution)/shard_map/tks,tkv->tsv/dot_general | solution.py:80
  99.2 2.5 multiply_reduce_fusion.3
  101.8 7.5 %fusion.16 = f32[26,128,512]{2,1,0:T(8,128)} fusion(f32[26,32,512]{2,1,0:T(8,128)S(1)} %get-tuple-element.21, f32[26,32,128]{2,1,0:T(8,128)S(1)} %copy-done.2, f32[26,128]{1,0:T(8,128)S(1)} %convert_element_type.70), kind=kOutput, calls=%fused_computation.30 | convolution fusion | flops 654417920 | bytes 8958976 | tf_op jit(solution)/shard_map/tks,tkg->tsg/dot_general | solution.py:82
  109.3 58.5 %all-gather.3.cloned.1.call-done = bf16[104,128,128]{2,1,0:T(8,128)(2,1)} async-done(((bf16[26,128,128]{2,1,0:T(8,128)(2,1)}), bf16[104,128,128]{2,1,0:T(8,128)(2,1)}) %all-gather.3.cloned.1.call-update) | async-done | bytes 3407888 | tf_op jit(solution)/shard_map/all_gather | solution.py:84
  167.8 10.3 %convert_bitcast_fusion = bf16[4,26,128,512]{2,3,0,1:T(8,128)(2,1)} fusion(f32[26,128,512]{2,1,0:T(8,128)} %fusion.16, bf16[26,128,512]{2,1,0:T(8,128)(2,1)S(1)} %copy-done, bf16[4,26,128,128]{3,2,1,0:T(8,128)(2,1)} %bitcast.42, f32[26,512]{1,0:T(8,128)S(1)} %rsqrt_multiply_fusion, f32[26,128]{1,0:T(8,128)S(1)} %convert_element_type.70), kind=kOutput, calls=%fused_computation | convolution fusion | flops 1760165888 | bytes 27329536 | tf_op jit(solution)/shard_map/ntsv,tsg->ntvg/dot_general | solution.py:85
  178.1 17.5 %copy.41 = bf16[4,26,128,512]{3,2,1,0:T(8,128)(2,1)} copy(bf16[4,26,128,512]{2,3,0,1:T(8,128)(2,1)} %convert_bitcast_fusion) | data formatting | bytes 27262976 | tf_op jit(solution)/shard_map/convert_element_type | solution.py:87
  195.7 104.4 %reduce-scatter.2.cloned.1.call-done = bf16[26,128,512]{2,1,0:T(8,128)(2,1)} async-done(((bf16[104,128,512]{2,1,0:T(8,128)(2,1)}), bf16[26,128,512]{2,1,0:T(8,128)(2,1)}) %reduce-scatter.2.cloned.1.call-update) | async-done | bytes 3407888 | tf_op jit(solution)/shard_map/reduce_scatter | solution.py:89
  300.1 2.4 constant_dynamic-slice_fusion
  302.4 1.7 collective-permute-start
  305.6 1.0 copy.50
  306.6 35.0 %collective-permute-done = bf16[1,26,64,512]{3,2,1,0:T(8,128)(2,1)} collective-permute-done((bf16[1,26,64,512]{3,2,1,0:T(8,128)(2,1)S(1)}, bf16[1,26,64,512]{3,2,1,0:T(8,128)(2,1)}, u32[]{:S(2)}, u32[]{:S(2)}) %collective-permute-start) | collective-permute-done | bytes 1703968 | tf_op jit(solution)/shard_map/ppermute | solution.py:95
  341.6 2.4 copy.43
  344.0 4.5 %multiply_reduce_fusion = (f32[64,512]{1,0:T(8,128)S(1)}, f32[64,512]{1,0:T(8,128)S(1)}) fusion(bf16[1,26,64,512]{3,1,2,0:T(8,128)(2,1)S(1)} %copy.43, bf16[1,26,64,512]{3,1,2,0:T(8,128)(2,1)S(1)} %bitcast.43, f32[52,26]{1,0:T(8,128)S(1)} %get-tuple-element.17, f32[52,26]{1,0:T(8,128)S(1)} %get-tuple-element.16, f32[52]{0:T(128)S(1)} %convert_element_type.68), kind=kOutput, calls=%fused_computation.1 | convolution fusion | flops 1075123456 | bytes 3681040 | tf_op jit(solution)/shard_map/ut,mtvg->umvg/dot_general | solution.py:98
  348.6 5.2 %collective-permute-start.1 = (bf16[2,64,512]{2,1,0:T(8,128)(2,1)S(1)}, bf16[2,64,512]{2,1,0:T(8,128)(2,1)S(1)}, u32[]{:S(2)}, u32[]{:S(2)}) collective-permute-start(bf16[2,64,512]{2,1,0:T(8,128)(2,1)S(1)} %pad_maximum_fusion), channel_id=1, source_target_pairs={{0,0},{1,4},{2,8},{3,12},{4,1},{5,5},{6,9},{7,13},{8,2},{9,6},{10,... | collective-permute-start | bytes 393224 | tf_op jit(solution)/shard_map/ppermute | solution.py:117
  353.8 1.5 collective-permute-start.2
  355.3 6.4 %collective-permute-done.1 = bf16[2,64,512]{2,1,0:T(8,128)(2,1)S(1)} collective-permute-done((bf16[2,64,512]{2,1,0:T(8,128)(2,1)S(1)}, bf16[2,64,512]{2,1,0:T(8,128)(2,1)S(1)}, u32[]{:S(2)}, u32[]{:S(2)}) %collective-permute-start.1) | collective-permute-done | bytes 131104 | tf_op jit(solution)/shard_map/ppermute | solution.py:117
  361.7 5.1 %collective-permute-done.2 = bf16[2,64,512]{2,1,0:T(8,128)(2,1)S(1)} collective-permute-done((bf16[2,64,512]{2,1,0:T(8,128)(2,1)S(1)}, bf16[2,64,512]{2,1,0:T(8,128)(2,1)S(1)}, u32[]{:S(2)}, u32[]{:S(2)}) %collective-permute-start.2) | collective-permute-done | bytes 131104 | tf_op jit(solution)/shard_map/ppermute | solution.py:118
  (39 shorter events, 2.3 us)
Async XLA Ops:
  7.2 11.7 %copy-start = (bf16[26,128,512]{2,1,0:T(8,128)(2,1)S(1)}, bf16[26,128,512]{2,1,0:T(8,128)(2,1)}, u32[]{:S(2)}) copy-start(bf16[26,128,512]{2,1,0:T(8,128)(2,1)} %param.7) | copy-start | bytes 10223620
  7.2 44.2 %all-reduce.6.cloned.1.call-start = ((), (), s32[]{:S(2)}) async-start(), calls=%async_computation.3 | async-start | bytes 607232 | tf_op jit(solution)/shard_map/psum | solution.py:68
  14.2 3.4 copy-start.3
  18.8 73.2 %all-reduce.8.cloned.1.call-start = ((), (), s32[]{:S(2)}) async-start(), calls=%async_computation.4 | async-start | bytes 2129920 | tf_op jit(solution)/shard_map/psum | solution.py:68
  18.8 6.2 %copy-start.1 = (f32[26,32,128]{2,1,0:T(8,128)S(1)}, f32[26,32,128]{2,1,0:T(8,128)}, u32[]{:S(2)}) copy-start(f32[26,32,128]{2,1,0:T(8,128)} %param.8) | copy-start | bytes 1277956
  18.9 6.2 %copy-start.4 = (bf16[26,128,128]{2,1,0:T(8,128)(2,1)S(1)}, bf16[26,128,128]{2,1,0:T(8,128)(2,1)}, u32[]{:S(2)}) copy-start(bf16[26,128,128]{2,1,0:T(8,128)(2,1)} %param.6) | copy-start | bytes 2555908
  27.4 140.4 %all-gather.3.cloned.1.call-start = ((), (), s32[]{:S(2)}) async-start(), calls=%async_computation.2 | async-start | bytes 4259840 | tf_op jit(solution)/shard_map/all_gather | solution.py:84
  51.4 42.2 %copy-start.7 = (bf16[26,128]{1,0:T(8,128)(2,1)S(1)}, bf16[26,128]{1,0:T(8,128)(2,1)}, u32[]{:S(2)}) copy-start(bf16[26,128]{1,0:T(8,128)(2,1)} %get-tuple-element.5) | copy-start | bytes 19972
  57.5 41.6 %copy-start.9 = (s32[52]{0:T(128)S(1)}, s32[52]{0:T(128)}, u32[]{:S(2)}) copy-start(s32[52]{0:T(128)} %param.10) | copy-start | bytes 628
  57.5 41.6 %copy-start.8 = (bf16[26]{0:T(256)(128)(2,1)S(1)}, bf16[26]{0:T(256)(128)(2,1)}, u32[]{:S(2)}) copy-start(bf16[26]{0:T(256)(128)(2,1)} %get-tuple-element.7) | copy-start | bytes 160
  93.6 8.2 %copy-start.6 = (bf16[26,512]{1,0:T(8,128)(2,1)S(1)}, bf16[26,512]{1,0:T(8,128)(2,1)}, u32[]{:S(2)}) copy-start(bf16[26,512]{1,0:T(8,128)(2,1)} %get-tuple-element.6) | copy-start | bytes 79876
  99.0 201.1 %reduce-scatter.2.cloned.1.call-start = ((), (), s32[]{:S(2)}) async-start(), calls=%async_computation.1 | async-start | bytes 17039360 | tf_op jit(solution)/shard_map/reduce_scatter | solution.py:89
  99.1 2.7 copy-start.2
  195.7 109.8 %copy-start.5 = (f32[52,52]{1,0:T(8,128)S(1)}, f32[52,52]{1,0:T(8,128)}, u32[]{:S(2)}) copy-start(f32[52,52]{1,0:T(8,128)} %param.11) | copy-start | bytes 32452
  302.4 39.1 %collective-permute-start = (bf16[1,26,64,512]{3,2,1,0:T(8,128)(2,1)S(1)}, bf16[1,26,64,512]{3,2,1,0:T(8,128)(2,1)}, u32[]{:S(2)}, u32[]{:S(2)}) collective-permute-start(bf16[1,26,64,512]{3,2,1,0:T(8,128)(2,1)S(1)} %get-tuple-element.11), channel_id=1, source_target_pairs={{0,16},{16,0},{1,17},{17,1},{2,18},{18,2},{3,19},{19,3},{4,20},{20... | collective-permute-start | bytes 5111816 | tf_op jit(solution)/shard_map/ppermute | solution.py:95
  348.6 13.1 %collective-permute-start.1 = (bf16[2,64,512]{2,1,0:T(8,128)(2,1)S(1)}, bf16[2,64,512]{2,1,0:T(8,128)(2,1)S(1)}, u32[]{:S(2)}, u32[]{:S(2)}) collective-permute-start(bf16[2,64,512]{2,1,0:T(8,128)(2,1)S(1)} %pad_maximum_fusion), channel_id=1, source_target_pairs={{0,0},{1,4},{2,8},{3,12},{4,1},{5,5},{6,9},{7,13},{8,2},{9,6},{10,... | collective-permute-start | bytes 393224 | tf_op jit(solution)/shard_map/ppermute | solution.py:117
  353.8 13.0 %collective-permute-start.2 = (bf16[2,64,512]{2,1,0:T(8,128)(2,1)S(1)}, bf16[2,64,512]{2,1,0:T(8,128)(2,1)S(1)}, u32[]{:S(2)}, u32[]{:S(2)}) collective-permute-start(bf16[2,64,512]{2,1,0:T(8,128)(2,1)S(1)} %pad_maximum_fusion), channel_id=1, source_target_pairs={{0,16},{1,20},{2,24},{3,28},{4,17},{5,21},{6,25},{7,29},{8,18},{9,... | collective-permute-start | bytes 393224 | tf_op jit(solution)/shard_map/ppermute | solution.py:118
Sparse Core Ops, SparseCore 0:
  18.9 32.4 all-reduce.5
  54.4 37.5 all-reduce.7
  99.1 68.6 all-gather.2
  195.8 104.2 reduce-scatter.1
